TPU v7x, 768 devices: a whole 4x8x12 slice. The times are simulated.
768 devices in a mesh: fsdp: 192 (over x, z, y_lo, core), island: 4 (over y_hi).
Axes of the slice: x: 4, y: 8 (y_hi: 4, y_lo: 2; y = y_hi * 2 + y_lo), z: 12, core: 2. Of those that a mesh axis runs over, the one named last changes fastest.
Arguments:
- activations: bfloat16 [4, 24576, 4224], P('island', 'fsdp'), may hold values from -24 to 24
- out_grads: bfloat16 [4, 24576, 512], P('island', 'fsdp'), may hold values from -0.038085938 to 0.038085938
- projection: bfloat16 [4224, 256], P('fsdp'), may hold values from -0.09375 to 0.09375
- first_moment: float32 [4, 1, 256, 512], P('island'), may hold values from -1.8 to 1.8
- second_moment: float32 [4, 1, 256, 512], P('island'), may hold values from 0.01 to 1
- inner_weights: float32 [4, 4224, 512], P('island', 'fsdp'), may hold values from -6 to 6
- global_weights: float32 [4224, 512], P('fsdp'), may hold values from -6 to 6
- outer_momentum: float32 [4224, 512], P('fsdp'), may hold values from -6 to 6
Outputs:
- new_weights: bfloat16 [4224, 512], P('fsdp', 'island')
- new_momentum: float32 [4224, 512], P('fsdp')
- new_first: float32 [4, 1, 256, 512], P('island')
- new_second: float32 [4, 1, 256, 512], P('island')
All inputs are finite; a program needn't handle non-finite values.
Results may differ from a plain program's by a relative error of at most 0.001.
Values sent between devices are 32-bit elements; how exact they have to be, the bound alone decides.
A program may use at most 64 MiB of HBM per device.

v0:
```python
import jax
import jax.numpy as jnp
from jax import lax
from jax.sharding import Mesh
from jax.sharding import PartitionSpec as P

DW = 4224
RANK = 256
LAYERS = 1
FSDP = ("fsdp_0", "fsdp_1", "fsdp_2", "fsdp_3")


first_decay = 0.9
second_decay = 0.999
first_fix = 1.0 - 0.9**10
second_fix = 1.0 - 0.999**10
epsilon = 1e-08
inner_rate = 1.0
outer_rate = 0.7
outer_beta = 0.9


def split_up(value, dim, length):
    before, after = (value.shape[:dim], value.shape[dim + 1 :])
    return jnp.moveaxis(value.reshape(*before, length, -1, *after), dim, 0)


def scatter_pairs(value, chips, core, dim):
    sizes = (lax.axis_size(chips), lax.axis_size(core))
    blocks = split_up(value, dim, sizes[0] * sizes[1])
    inside = blocks.shape[1:]
    blocks = blocks.reshape(*sizes, *inside).swapaxes(0, 1).reshape(-1, *inside)
    blocks = lax.psum_scatter(blocks, core, scatter_dimension=0, tiled=True)
    return lax.psum_scatter(blocks, chips, scatter_dimension=0, tiled=True)[0]


def rows_for(lines, length):
    spare = -lines.shape[0] % length
    if not spare:
        return lines
    return jnp.concatenate([lines, jnp.zeros((spare, *lines.shape[1:]), lines.dtype)])


def nested_sum(value, near, far):
    lines = value.reshape(-1, *value.shape[1:][-1:])
    padded = rows_for(lines, lax.axis_size(near))
    own = lax.psum_scatter(padded, near, scatter_dimension=0, tiled=True)
    own = lax.psum(own, far)
    whole = lax.all_gather(own, near, axis=0, tiled=True)
    return whole[: len(lines)].reshape(value.shape)


def gathered_total(value, axis):
    blocks = lax.all_gather(value, axis)
    return blocks.sum(axis=0)


def layer_select(first_row, row_count):
    layer_of = (first_row + lax.iota(jnp.int32, row_count)) // DW
    return (layer_of[:, None] == lax.iota(jnp.int32, LAYERS)[None, :]).astype(jnp.float32)


def outer_step(stepped_sum, global_part, momentum_part, island_count):
    pseudo_grad = global_part - stepped_sum / island_count
    momentum_next = outer_beta * momentum_part + pseudo_grad
    weights_next = (global_part - outer_rate * (pseudo_grad + outer_beta * momentum_next)).astype(
        jnp.bfloat16
    )
    return (weights_next, momentum_next)


def body(
    activations,
    out_grads,
    projection,
    first_moment,
    second_moment,
    inner_weights,
    global_weights,
    outer_momentum,
):
    inputs = activations[0]
    grads_out = out_grads[0]
    row_count = projection.shape[0]
    col_total = global_weights.shape[1]
    product = lax.dot_general(
        inputs, grads_out, (((0,), (0,)), ((), ())), preferred_element_type=jnp.float32
    )
    grad_rows = scatter_pairs(product, ("fsdp_0", "fsdp_1", "fsdp_2"), "fsdp_3", 0)
    first_row = lax.axis_index(FSDP) * row_count
    select = layer_select(first_row, row_count)
    lifted = (projection.astype(jnp.float32)[:, None, :] * select[:, :, None]).reshape(
        row_count, LAYERS * RANK
    )
    partial_sum = lax.dot_general(
        lifted,
        grad_rows,
        (((0,), (0,)), ((), ())),
        precision=lax.Precision.HIGHEST,
        preferred_element_type=jnp.float32,
    )
    projected = nested_sum(partial_sum, "fsdp_3", ("fsdp_0", "fsdp_1", "fsdp_2")).reshape(
        LAYERS, RANK, col_total
    )
    new_first = first_decay * first_moment[0] + (1.0 - first_decay) * projected
    new_second = second_decay * second_moment[0] + (1.0 - second_decay) * projected * projected
    adapted = new_first / first_fix / (jnp.sqrt(new_second / second_fix) + epsilon)
    channel_scale = jnp.sqrt(jnp.mean(adapted * adapted, axis=1)) / jnp.sqrt(
        jnp.mean(projected * projected, axis=1) + 1e-06
    )
    row_scale = jnp.sum(select[:, :, None] * channel_scale[None, :, :], axis=1)
    stepped = inner_weights[0] - inner_rate * grad_rows * row_scale
    island_count = lax.axis_size("island")
    block_cols = col_total // island_count
    block_start = lax.axis_index("island") * block_cols
    island_total = gathered_total(stepped, "island")
    weights_next, new_momentum = outer_step(
        island_total, global_weights, outer_momentum, island_count
    )
    weights_block = lax.dynamic_slice_in_dim(weights_next, block_start, block_cols, 1)
    return (weights_block, new_momentum, new_first[None], new_second[None])


def solution(mesh):
    torus = Mesh(
        mesh.devices.reshape(4, 12, 2, 2, mesh.shape["island"]),
        ("fsdp_0", "fsdp_1", "fsdp_2", "fsdp_3", "island"),
    )
    placed = (
        P("island", FSDP, None),
        P("island", FSDP, None),
        P(FSDP, None),
        P("island", None, None, None),
        P("island", None, None, None),
        P("island", FSDP, None),
        P(FSDP, None),
        P(FSDP, None),
    )
    return jax.shard_map(
        body,
        mesh=torus,
        in_specs=placed,
        out_specs=(
            P(FSDP, "island"),
            P(FSDP, None),
            P("island", None, None, None),
            P("island", None, None, None),
        ),
        check_vma=False,
    )
```

profile of v0, /device:TPU:1, one launch (start us, length us, event | category | flops | bytes accessed | tf_op | source)
XLA Modules:
  0.0 1833.1 jit_solution(6971225878803386230)
XLA Ops:
  7.2 0.0 copy-start
  7.2 0.0 reduce-scatter.4.cloned.1.call-start
  7.2 1.9 copy.16
  9.1 0.3 dot_general.11
  9.5 0.0 copy-done
  9.5 1.3 convolution_bitcast_fusion
  10.7 4.3 copy.18
  15.1 0.0 reduce-scatter.4.cloned.1.call-update
  15.1 0.0 copy-start.7
  15.1 0.0 copy-start.1
  15.1 0.0 copy-start.2
  15.1 0.0 all-reduce.6.cloned.1.call-start
  15.2 36.8 %reduce-scatter.4.cloned.1.call-done = f32[96,22,512]{2,0,1:T(8,128)} async-done(((f32[192,22,512]{2,0,1:T(8,128)}), f32[96,22,512]{2,0,1:T(8,128)}) %reduce-scatter.4.cloned.1.call-update) | async-done | bytes 4325392 | tf_op jit(solution)/shard_map/reduce_scatter | solution.py:33
  52.0 0.0 copy-start.6
  52.0 0.0 copy-start.3
  52.0 0.0 copy-start.5
  52.0 0.0 all-reduce.6.cloned.1.call-update
  52.0 0.0 reduce-scatter.6.cloned.1.call-start
  52.1 1.3 dynamic-slice
  53.3 847.8 %all-reduce.6.cloned.1.call-done = f32[96,22,512]{2,0,1:T(8,128)} async-done(((f32[96,22,512]{2,0,1:T(8,128)}), f32[96,22,512]{2,0,1:T(8,128)}) %all-reduce.6.cloned.1.call-update) | async-done | bytes 4325392
  901.1 1.7 constant_dynamic-slice_fusion
  902.8 0.0 copy-done.7
  902.8 1.5 fusion.5
  904.3 0.0 reduce-scatter.6.cloned.1.call-update
  904.3 0.0 all-reduce.4.cloned.1.call-start
  904.4 79.9 %reduce-scatter.6.cloned.1.call-done = f32[128,512]{1,0:T(8,128)} async-done(((f32[256,512]{1,0:T(8,128)}), f32[128,512]{1,0:T(8,128)}) %reduce-scatter.6.cloned.1.call-update) | async-done | bytes 262160 | tf_op jit(solution)/shard_map/reduce_scatter | solution.py:47
  984.3 0.0 all-reduce.4.cloned.1.call-update
  984.3 776.3 %all-reduce.4.cloned.1.call-done = f32[128,512]{1,0:T(8,128)} async-done(((f32[128,512]{1,0:T(8,128)}), f32[128,512]{1,0:T(8,128)}) %all-reduce.4.cloned.1.call-update) | async-done | bytes 262160 | tf_op jit(solution)/shard_map/psum | solution.py:48
  1760.6 49.4 %all_gather.7 = f32[256,512]{1,0:T(8,128)S(1)} all-gather(f32[128,512]{1,0:T(8,128)} %all-reduce.4.cloned.1.call-done), channel_id=1, replica_groups=mesh['fsdp_0'=4,'fsdp_1'=12,'fsdp_2'=2,'fsdp_3'=2,'island'=4] {'fsdp_3'}, dimensions={0}, use_global_device_ids=true | all-gather | bytes 786432 | tf_op jit(solution)/shard_map/all_gather | solution.py:49
  1810.0 0.0 copy-done.1
  1810.0 0.0 copy-done.2
  1810.0 1.4 multiply_reduce_fusion.1
  1811.4 0.0 copy-done.6
  1811.4 1.7 multiply_subtract_fusion.1
  1813.2 12.7 all_gather.8
  1825.9 0.0 copy-done.3
  1825.9 0.0 copy-done.5
  1826.0 0.0 copy-start.4
  1826.0 0.6 fusion.10
  1826.6 0.0 copy-done.4
  (5 shorter events, 0.1 us)
Async XLA Ops:
  7.2 2.3 copy-start
  7.2 44.8 %reduce-scatter.4.cloned.1.call-start = ((), (), s32[]{:S(2)}) async-start(), calls=%async_computation.2 | async-start | bytes 12976128 | tf_op jit(solution)/shard_map/reduce_scatter | solution.py:33
  15.1 887.7 %copy-start.7 = (bf16[22,256]{1,0:T(8,128)(2,1)S(1)}, bf16[22,256]{1,0:T(8,128)(2,1)}, u32[]{:S(2)}) copy-start(bf16[22,256]{1,0:T(8,128)(2,1)} %param.10) | copy-start | bytes 33796
  15.1 1794.9 %copy-start.1 = (f32[1,1,256,512]{3,2,1,0:T(8,128)S(1)}, f32[1,1,256,512]{3,2,1,0:T(8,128)}, u32[]{:S(2)}) copy-start(f32[1,1,256,512]{3,2,1,0:T(8,128)} %param.11) | copy-start | bytes 1572868
  15.1 1794.9 %copy-start.2 = (f32[1,1,256,512]{3,2,1,0:T(8,128)S(1)}, f32[1,1,256,512]{3,2,1,0:T(8,128)}, u32[]{:S(2)}) copy-start(f32[1,1,256,512]{3,2,1,0:T(8,128)} %param.12) | copy-start | bytes 1572868
  15.1 886.0 %all-reduce.6.cloned.1.call-start = ((), (), s32[]{:S(2)}) async-start(), calls=%async_computation.5 | async-start | bytes 8650752
  52.0 1759.5 %copy-start.6 = (f32[1,22,512]{2,0,1:T(1,128)S(1)}, f32[1,22,512]{2,0,1:T(1,128)}, u32[]{:S(2)}) copy-start(f32[1,22,512]{2,0,1:T(1,128)} %param.13) | copy-start | bytes 135172
  52.0 1774.0 %copy-start.3 = (f32[22,512]{1,0:T(8,128)S(1)}, f32[22,512]{1,0:T(8,128)}, u32[]{:S(2)}) copy-start(f32[22,512]{1,0:T(8,128)} %param.14) | copy-start | bytes 135172
  52.0 1774.0 %copy-start.5 = (f32[22,512]{1,0:T(8,128)S(1)}, f32[22,512]{1,0:T(8,128)}, u32[]{:S(2)}) copy-start(f32[22,512]{1,0:T(8,128)} %param.15) | copy-start | bytes 135172
  52.0 932.3 %reduce-scatter.6.cloned.1.call-start = ((), (), s32[]{:S(2)}) async-start(), calls=%async_computation.3 | async-start | bytes 786432 | tf_op jit(solution)/shard_map/reduce_scatter | solution.py:47
  904.3 856.3 %all-reduce.4.cloned.1.call-start = ((), (), s32[]{:S(2)}) async-start(), calls=%async_computation.4 | async-start | bytes 524288 | tf_op jit(solution)/shard_map/psum | solution.py:48
  1826.0 0.6 copy-start.4
Sparse Core Ops, SparseCore 0:
  15.2 36.6 reduce-scatter.3
  55.2 845.9 all-reduce.5
  904.8 79.4 reduce-scatter.5
  987.3 773.2 all-reduce.3
where the time goes:
time: 1830 us
  waiting for transfers between devices  1740 us (95%)
  blocking collectives  62.1 us (3%)
    unnamed x5, waiting for transfers between devices  848 us
    psum x1, waiting for transfers between devices, nested_sum(): own = lax.psum(own, far)  776 us
    reduce_scatter x1, waiting for transfers between devices, nested_sum(): own = lax.psum_scatter(padded, near, scatter_dimension=0, tiled=True)  79.9 us
    all_gather x1, blocking collectives, nested_sum(): whole = lax.all_gather(own, near, axis=0, tiled=True)  49.4 us
    reduce_scatter x1, waiting for transfers between devices, scatter_pairs(): blocks = lax.psum_scatter(blocks, core, scatter_dimension=0, tiled=True)  36.8 us
  transfers between devices with their start and end apart: 4, of which 4 were waited for; matrix products, arithmetic and copies ran while one was open for 0% of the time, Pallas kernels for 0%

commit v1 on v0

v1 whole, which is shorter than its diff:
```python
import functools

import jax
import jax.numpy as jnp
from jax import lax
from jax.experimental import pallas as pl
from jax.experimental.pallas import tpu as pltpu
from jax.sharding import Mesh
from jax.sharding import PartitionSpec as P

RANK = 256
X, Z, Y, C = "fsdp_0", "fsdp_1", "fsdp_2", "fsdp_3"
ISLAND = "island"
FSDP = (X, Z, Y, C)
LANES = 128
MESH_ID = pl.DeviceIdType.MESH
F32 = jnp.float32

first_decay = 0.9
second_decay = 0.999
first_fix = 1.0 - 0.9**10
second_fix = 1.0 - 0.999**10
epsilon = 1e-08
inner_rate = 1.0
outer_rate = 0.7
outer_beta = 0.9


class Lanes:
    def __init__(self, send_sems, recv_sems):
        self.send_sems, self.recv_sems = send_sems, recv_sems
        self.used = 0
        self.started = []

    def send(self, src, dst, **peer):
        copy = pltpu.make_async_remote_copy(
            src_ref=src,
            dst_ref=dst,
            send_sem=self.send_sems.at[self.used],
            recv_sem=self.recv_sems.at[self.used],
            device_id=peer,
            device_id_type=MESH_ID,
        )
        self.used += 1
        copy.start()
        self.started.append(copy)
        return copy


def turn(axis, by):
    size = lax.axis_size(axis)
    return lax.rem(lax.axis_index(axis) + by + size, size)


def chain(lanes, axis, steps, way, block, slots):
    copy = None
    for step in range(steps):
        at = block(turn(axis, way * (steps - step)))
        if copy is not None:
            copy.wait_recv()
            at[...] = at[...] + slots[step - 1]
        copy = lanes.send(at, slots.at[step], **{axis: turn(axis, way)})
        yield
    copy.wait_recv()
    at = block(lax.axis_index(axis))
    at[...] = at[...] + slots[steps - 1]


def advance(chains):
    for one in chains:
        next(one, None)


def comm_kernel(
    a_ref, g_ref, p_ref, first_ref, second_ref, w_ref,
    proj_ref, total_ref,
    a_out, a_in, g_out, g_in, p_out, p_in, p_all,
    part_z, part_x,
    z_up, z_down, x_up, x_down, zx_up, zx_down, xz_up, xz_down,
    y_z, y_x, grad, grad_own, w_all, grad_all,
    proj_part, proj_x, proj_z, proj_all, stats, scales, scale_all,
    send_sems, recv_sems,
):
    xk, zk, yk, ck = (lax.axis_index(name) for name in FSDP)
    island = lax.axis_index(ISLAND)
    nx, nz = lax.axis_size(X), lax.axis_size(Z)
    ni = lax.axis_size(ISLAND)
    lanes = Lanes(send_sems, recv_sems)
    other_c, other_y = 1 - ck, 1 - yk
    quad = yk * 2 + ck
    half = g_ref.shape[1] // 2
    rows = p_ref.shape[0]
    mine = pl.ds(pl.multiple_of(ck * half, half), half)
    theirs = pl.ds(pl.multiple_of(other_c * half, half), half)

    barrier = pltpu.get_barrier_semaphore()
    partners = [{C: other_c}, {Y: other_y}, {Y: other_y, C: other_c}]
    partners += [{X: turn(X, by)} for by in range(1, nx)]
    partners += [{Z: turn(Z, 1)}, {Z: turn(Z, -1)}]
    partners += [{ISLAND: turn(ISLAND, by)} for by in range(1, ni)]
    for partner in partners:
        pl.semaphore_signal(barrier, inc=1, device_id=partner, device_id_type=MESH_ID)
    a_out[...] = a_ref[...].astype(F32)
    g_out[...] = g_ref[:, theirs].astype(F32)
    p_out[...] = p_ref[...].astype(F32)
    pl.semaphore_wait(barrier, len(partners))

    got_g = lanes.send(g_out, g_in, **{C: other_c})
    got_a = lanes.send(a_out, a_in, **{C: other_c})
    got_p = [lanes.send(p_out, p_in.at[quad], **peer) for peer in partners[:3]]
    got_w = [
        lanes.send(w_ref, w_all.at[island], **{ISLAND: turn(ISLAND, by)})
        for by in range(1, ni)
    ]

    def product(a, g, add):
        wide = 11 * LANES
        count = wide // part_z.shape[2]
        for at in range(a.shape[1] // wide):
            lhs = a[:, at * wide : (at + 1) * wide].astype(jnp.bfloat16)
            out = lax.dot_general(
                lhs, g, (((0,), (0,)), ((), ())), preferred_element_type=F32
            )
            out = out.reshape(count, part_z.shape[2], half)
            block = at * count
            done = 0
            while done < count:
                x, z = divmod(block + done, nz)
                take = min(nz - z, count - done)
                for ref, cols in ((part_z, slice(0, LANES)), (part_x, slice(LANES, half))):
                    piece = out[done : done + take, :, cols]
                    if add:
                        piece = ref[x, z : z + take] + piece
                    ref[x, z : z + take] = piece
                done += take

    product(a_ref, g_ref[:, mine], False)
    p_in[quad] = p_out[...]
    got_g.wait_recv()
    got_a.wait_recv()
    product(a_in, g_in[...].astype(jnp.bfloat16), True)

    up_z, up_x = nz // 2, nx // 2
    first_z, first_x = [], []
    for sub in range(2):
        lead_z, lead_x = pl.ds(sub * (nx // 2), nx // 2), pl.ds(sub * (nz // 2), nz // 2)
        at_z = lambda d, lead=lead_z: part_z.at[lead, d]
        at_x = lambda d, lead=lead_x: part_x.at[d, lead]
        for way, z_slots, x_slots in ((1, z_up, x_up), (-1, z_down, x_down)):
            less = int((way == 1) == (sub == 1))
            first_z.append(chain(lanes, Z, up_z - less, way, at_z, z_slots.at[sub]))
            first_x.append(chain(lanes, X, up_x - less, way, at_x, x_slots.at[sub]))
    second_z = [
        chain(lanes, Z, up_z, 1, lambda d: part_x.at[xk, d], xz_up),
        chain(lanes, Z, up_z - 1, -1, lambda d: part_x.at[xk, d], xz_down),
    ]
    second_x = [
        chain(lanes, X, up_x, 1, lambda d: part_z.at[d, zk], zx_up),
        chain(lanes, X, up_x - 1, -1, lambda d: part_z.at[d, zk], zx_down),
    ]
    advance(first_z)
    advance(first_x)
    advance(first_z)
    advance(first_z)
    advance(first_x)
    advance(first_z)
    advance(first_z)
    advance(first_x)
    advance(second_z)
    advance(first_z)
    advance(second_z)
    advance(first_z)
    advance(second_x)
    advance(second_z)
    advance(second_x)
    advance(second_z)
    advance(second_x)
    got_yz = lanes.send(part_z.at[xk, zk], y_z, **{Y: other_y})
    for _ in range(3):
        advance(second_z)
    got_yx = lanes.send(part_x.at[xk, zk], y_x, **{Y: other_y})

    for j, copy in enumerate(got_p):
        copy.wait_recv()
    for j in range(4):
        p_all[j * rows : (j + 1) * rows, :] = p_in[j]

    got_yz.wait_recv()
    got_yx.wait_recv()
    grad[:, mine] = jnp.concatenate(
        [part_z[xk, zk] + y_z[...], part_x[xk, zk] + y_x[...]], axis=1
    )
    got_grad = lanes.send(grad.at[:, mine], grad.at[:, mine], **{C: other_c})

    proj_part[...] = lax.dot_general(
        p_all[...],
        grad[:, mine],
        (((0,), (0,)), ((), ())),
        precision=lax.Precision.HIGHEST,
        preferred_element_type=F32,
    ).reshape(proj_part.shape)
    got_x = [
        lanes.send(proj_part.at[turn(X, by)], proj_x.at[by - 1], **{X: turn(X, by)})
        for by in range(1, nx)
    ]

    got_grad.wait_recv()
    for j in range(4):
        @pl.when(quad == j)
        def _(j=j):
            grad_own[...] = grad[j * rows : (j + 1) * rows, :]
    got_gi = [
        lanes.send(grad_own, grad_all.at[island], **{ISLAND: turn(ISLAND, by)})
        for by in range(1, ni)
    ]

    own = proj_part[xk]
    for copy, by in zip(got_x, range(1, nx)):
        copy.wait_recv()
        own = own + proj_x[by - 1]
    proj_z[zk] = own

    ups, downs = [], []
    for step in range(up_z):
        for way, held, last in ((1, ups, up_z), (-1, downs, up_z - 1)):
            if step >= last:
                continue
            if held:
                held[-1].wait_recv()
            source = proj_z.at[turn(Z, -way * step)]
            held.append(lanes.send(source, source, **{Z: turn(Z, way)}))
    ups[-1].wait_recv()
    downs[-1].wait_recv()
    block = proj_z[0]
    for z in range(1, nz):
        block = block + proj_z[z]
    depth = block.shape[0]
    here = pl.ds(pl.multiple_of(xk * depth, depth), depth)
    new_first = first_decay * first_ref[here, mine] + (1.0 - first_decay) * block
    new_second = second_decay * second_ref[here, mine] + (1.0 - second_decay) * block * block
    adapted = new_first / first_fix / (jnp.sqrt(new_second / second_fix) + epsilon)
    stats[xk, 0:1] = jnp.sum(adapted * adapted, axis=0, keepdims=True)
    stats[xk, 1:2] = jnp.sum(block * block, axis=0, keepdims=True)
    got_stats = [
        lanes.send(stats.at[xk], stats.at[xk], **{X: turn(X, by)}) for by in range(1, nx)
    ]
    proj_all[xk, :, mine] = block
    got_proj = [
        lanes.send(
            proj_all.at[xk, :, mine], proj_all.at[xk, :, mine], **{X: turn(X, by)}
        )
        for by in range(1, nx)
    ]
    for copy in got_stats:
        copy.wait_recv()
    sums = stats[0]
    for x in range(1, nx):
        sums = sums + stats[x]
    sums = sums / RANK
    scales[ck] = jnp.sqrt(sums[0:1]) / jnp.sqrt(sums[1:2] + 1e-06)
    got_scale = lanes.send(scales.at[ck], scales.at[ck], **{C: other_c})
    got_scale.wait_recv()
    for core in range(2):
        scale_all[island, :, core * half : (core + 1) * half] = scales[core]
    got_si = [
        lanes.send(
            scale_all.at[island], scale_all.at[island], **{ISLAND: turn(ISLAND, by)}
        )
        for by in range(1, ni)
    ]

    for copy in got_proj:
        copy.wait_recv()
    got_half = lanes.send(
        proj_all.at[:, :, mine], proj_all.at[:, :, mine], **{C: other_c}
    )
    w_all[island] = w_ref[...]
    grad_all[island] = grad_own[...]
    for copy in got_w + got_gi:
        copy.wait_recv()
    got_half.wait_recv()
    proj_ref[...] = proj_all[...].reshape(proj_ref.shape)
    for copy in got_si:
        copy.wait_recv()
    total = None
    for i in range(ni):
        stepped = w_all[i] - inner_rate * grad_all[i] * scale_all[i]
        total = stepped if total is None else total + stepped
    total_ref[...] = total
    for copy in lanes.started:
        copy.wait_send()


def exchange(a, g, p, first, second, w):
    tokens, features = a.shape
    cols = g.shape[1]
    half = cols // 2
    rows = p.shape[0]
    nx, nz, ni = lax.axis_size(X), lax.axis_size(Z), lax.axis_size(ISLAND)
    quad = 4 * rows
    ups, downs = nz // 2, nz // 2 - 1
    vmem = lambda *shape: pltpu.VMEM(shape, F32)
    depth = RANK // nx
    scratch = [
        vmem(tokens, features), vmem(tokens, features),
        vmem(tokens, half), vmem(tokens, half),
        vmem(rows, RANK), vmem(4, rows, RANK), vmem(quad, RANK),
        vmem(nx, nz, quad, LANES), vmem(nx, nz, quad, LANES),
        vmem(2, ups, nx // 2, quad, LANES), vmem(2, ups, nx // 2, quad, LANES),
        vmem(2, nx // 2, nz // 2, quad, LANES), vmem(2, nx // 2, nz // 2, quad, LANES),
        vmem(nx // 2, quad, LANES), vmem(nx // 2, quad, LANES),
        vmem(ups, quad, LANES), vmem(ups, quad, LANES),
        vmem(quad, LANES), vmem(quad, LANES),
        vmem(quad, cols), vmem(rows, cols), vmem(ni, rows, cols), vmem(ni, rows, cols),
        vmem(nx, depth, half), vmem(nx - 1, depth, half), vmem(nz, depth, half),
        vmem(nx, depth, cols), vmem(nx, 2, half), vmem(2, 1, half), vmem(ni, 1, cols),
        pltpu.SemaphoreType.DMA((96,)),
        pltpu.SemaphoreType.DMA((96,)),
    ]
    return pl.pallas_call(
        comm_kernel,
        name="exchange",
        out_shape=(
            jax.ShapeDtypeStruct((RANK, cols), F32),
            jax.ShapeDtypeStruct((rows, cols), F32),
        ),
        in_specs=[pl.BlockSpec(memory_space=pltpu.VMEM)] * 6,
        out_specs=(pl.BlockSpec(memory_space=pltpu.VMEM),) * 2,
        scratch_shapes=scratch,
        compiler_params=pltpu.CompilerParams(
            collective_id=0, has_side_effects=True, vmem_limit_bytes=48 << 20
        ),
    )(a, g, p, first, second, w)


def body(
    activations,
    out_grads,
    projection,
    first_moment,
    second_moment,
    inner_weights,
    global_weights,
    outer_momentum,
):
    projected, stepped_sum = exchange(
        activations[0],
        out_grads[0],
        projection,
        first_moment[0, 0],
        second_moment[0, 0],
        inner_weights[0],
    )
    new_first = first_decay * first_moment[0, 0] + (1.0 - first_decay) * projected
    new_second = (
        second_decay * second_moment[0, 0] + (1.0 - second_decay) * projected * projected
    )
    island_count = lax.axis_size(ISLAND)
    pseudo_grad = global_weights - stepped_sum / island_count
    new_momentum = outer_beta * outer_momentum + pseudo_grad
    weights_next = (
        global_weights - outer_rate * (pseudo_grad + outer_beta * new_momentum)
    ).astype(jnp.bfloat16)
    block_cols = global_weights.shape[1] // island_count
    weights_block = lax.dynamic_slice_in_dim(
        weights_next, lax.axis_index(ISLAND) * block_cols, block_cols, 1
    )
    return (weights_block, new_momentum, new_first[None, None], new_second[None, None])


def solution(mesh):
    torus = Mesh(
        mesh.devices.reshape(4, 12, 2, 2, mesh.shape["island"]),
        (*FSDP, ISLAND),
    )
    placed = (
        P(ISLAND, FSDP, None),
        P(ISLAND, FSDP, None),
        P(FSDP, None),
        P(ISLAND, None, None, None),
        P(ISLAND, None, None, None),
        P(ISLAND, FSDP, None),
        P(FSDP, None),
        P(FSDP, None),
    )
    return jax.shard_map(
        body,
        mesh=torus,
        in_specs=placed,
        out_specs=(
            P(FSDP, ISLAND),
            P(FSDP, None),
            P(ISLAND, None, None, None),
            P(ISLAND, None, None, None),
        ),
        check_vma=False,
    )
```

time: 1830 us -> 114 us (0.06)
  waiting for transfers between devices: 1740 us -> 0 us
  Pallas kernels: 0 us -> 106 us
  blocking collectives: 62.1 us -> 0 us
    unnamed x5 -> x0, waiting for transfers between devices: 848 us -> none
    psum x1 -> x0, waiting for transfers between devices: 776 us -> none  [nested_sum(): own = lax.psum(own, far)]
    reduce_scatter x2 -> x0, waiting for transfers between devices: 117 us -> none  [the longest x1 79.9 us: nested_sum(): own = lax.psum_scatter(padded, near, scatter_dimension=0, tiled=True)]
    pallas_call x0 -> x1, Pallas kernels: none -> 106 us  [exchange(): pl.pallas_call(comm_kernel, name='exchange', out_shape=(jax.ShapeDtypeStr...]
    all_gather x2 -> x0, blocking collectives: 62.1 us -> none  [the longest x1 49.4 us: nested_sum(): whole = lax.all_gather(own, near, axis=0, tiled=True)]
  transfers between devices with their start and end apart: 4 -> 0, of which waited for: 4 -> 0; matrix products, arithmetic and copies ran while one was open for 0% -> 0% of each run, Pallas kernels for 0% -> 0%
where the time goes in v1:
time: 114 us
  Pallas kernels  106 us (93%)
  local copies, waits for them, and re-layouts  5.74 us (5%)
  other arithmetic  1.79 us (2%)
    pallas_call x1, Pallas kernels, exchange(): pl.pallas_call(comm_kernel, name='exchange', out_shape=(jax.ShapeDtypeStr...  106 us
    unnamed x17, local copies, waits for them, and re-layouts  5.74 us

profile of v1, /device:TPU:1, one launch (start us, length us, event | category | flops | bytes accessed | tf_op | source)
XLA Modules:
  0.0 114.0 jit_solution(5754030954725409021)
XLA Ops:
  0.6 0.8 copy.14
  1.4 0.0 copy-start
  1.4 1.0 copy-done
  2.5 0.0 copy-start.1
  2.5 1.0 copy-done.1
  3.5 0.0 copy-start.2
  3.5 1.2 %copy-done.2 = bf16[1,128,4224]{2,1,0:T(8,128)(2,1)S(1)} copy-done((bf16[1,128,4224]{2,1,0:T(8,128)(2,1)S(1)}, bf16[1,128,4224]{2,1,0:T(8,128)(2,1)}, u32[]{:S(2)}) %copy-start.2) | copy-done | bytes 1081368
  4.7 0.0 copy-start.3
  4.8 0.9 copy-done.3
  5.7 0.0 copy-start.4
  5.7 0.7 copy-done.4
  6.4 0.0 copy-start.5
  6.4 0.0 copy-start.7
  6.4 105.8 %exchange.1 = (f32[256,512]{1,0:T(8,128)S(1)}, f32[22,512]{1,0:T(8,128)S(1)}) custom-call(bf16[128,4224]{1,0:T(8,128)(2,1)S(1)} %bitcast.15, bf16[128,512]{1,0:T(8,128)(2,1)S(1)} %bitcast.17, bf16[22,256]{1,0:T(8,128)(2,1)S(1)} %copy-done.4, f32[256,512]{1,0:T(8,128)S(1)} %bitcast.13, f32[256,512]{1,0:T(8,128)S(1)} %bitcast.14, f32[22,512]{1,0:T(8,128)S(1)} %bitcast.16), custom_call_target="tpu_custom_call" | custom-call | tf_op jit(solution)/shard_map/exchange/pallas_call | solution.py:320
  112.1 0.0 copy-done.5
  112.2 0.0 copy-done.7
  112.2 0.0 copy-start.6
  112.2 0.6 fusion.2
  112.8 1.2 %fusion.1 = (f32[1,1,256,512]{3,2,1,0:T(8,128)}, f32[1,1,256,512]{3,2,1,0:T(8,128)}) fusion(f32[256,512]{1,0:T(8,128)S(1)} %get-tuple-element.7, f32[1,1,256,512]{3,2,1,0:T(8,128)S(1)} %copy-done.1, f32[1,1,256,512]{3,2,1,0:T(8,128)S(1)} %copy-done), kind=kLoop, calls=%fused_computation.2 | loop fusion | flops 917504 | bytes 2621440 | tf_op jit(solution)/shard_map/broadcast_in_dim | solution.py:368
  114.0 0.0 copy-done.6
  (1 shorter events, 0.0 us)
Async XLA Ops:
  1.4 1.0 copy-start
  2.5 1.0 copy-start.1
  3.5 1.2 %copy-start.2 = (bf16[1,128,4224]{2,1,0:T(8,128)(2,1)S(1)}, bf16[1,128,4224]{2,1,0:T(8,128)(2,1)}, u32[]{:S(2)}) copy-start(bf16[1,128,4224]{2,1,0:T(8,128)(2,1)} %param.8) | copy-start | bytes 3244036
  4.7 0.9 copy-start.3
  5.7 0.7 copy-start.4
  6.4 105.8 %copy-start.5 = (f32[22,512]{1,0:T(8,128)S(1)}, f32[22,512]{1,0:T(8,128)}, u32[]{:S(2)}) copy-start(f32[22,512]{1,0:T(8,128)} %param.14) | copy-start | bytes 135172
  6.4 105.8 %copy-start.7 = (f32[22,512]{1,0:T(8,128)S(1)}, f32[22,512]{1,0:T(8,128)}, u32[]{:S(2)}) copy-start(f32[22,512]{1,0:T(8,128)} %param.15) | copy-start | bytes 135172
  112.2 1.8 %copy-start.6 = (f32[22,512]{1,0:T(8,128)}, f32[22,512]{1,0:T(8,128)S(1)}, u32[]{:S(2)}) copy-start(f32[22,512]{1,0:T(8,128)S(1)} %get-tuple-element.8) | copy-start | bytes 135172

commit v2 on v1

v2 whole, which is shorter than its diff:
```python
import functools

import jax
import jax.numpy as jnp
from jax import lax
from jax.experimental import pallas as pl
from jax.experimental.pallas import tpu as pltpu
from jax.sharding import Mesh
from jax.sharding import PartitionSpec as P

RANK = 256
X, Z, Y, C = "fsdp_0", "fsdp_1", "fsdp_2", "fsdp_3"
ISLAND = "island"
FSDP = (X, Z, Y, C)
LANES = 128
MESH_ID = pl.DeviceIdType.MESH
F32 = jnp.float32

first_decay = 0.9
second_decay = 0.999
first_fix = 1.0 - 0.9**10
second_fix = 1.0 - 0.999**10
epsilon = 1e-08
inner_rate = 1.0
outer_rate = 0.7
outer_beta = 0.9


class Lanes:
    def __init__(self, send_sems, recv_sems):
        self.send_sems, self.recv_sems = send_sems, recv_sems
        self.used = 0
        self.started = []

    def send(self, src, dst, **peer):
        copy = pltpu.make_async_remote_copy(
            src_ref=src,
            dst_ref=dst,
            send_sem=self.send_sems.at[self.used],
            recv_sem=self.recv_sems.at[self.used],
            device_id=peer,
            device_id_type=MESH_ID,
        )
        self.used += 1
        copy.start()
        self.started.append(copy)
        return copy


def turn(axis, by):
    size = lax.axis_size(axis)
    return lax.rem(lax.axis_index(axis) + by + size, size)


def chain(lanes, axis, steps, way, block, slots):
    copy = None
    for step in range(steps):
        at = block(turn(axis, way * (steps - step)))
        if copy is not None:
            copy.wait_recv()
            at[...] = at[...] + slots[step - 1]
        copy = lanes.send(at, slots.at[step], **{axis: turn(axis, way)})
        yield
    copy.wait_recv()
    at = block(lax.axis_index(axis))
    at[...] = at[...] + slots[steps - 1]


def advance(chains):
    for one in chains:
        next(one, None)


def comm_kernel(
    a_hbm, g_hbm, p_hbm, first_hbm, second_hbm, w_hbm,
    proj_ref, total_ref,
    a_ref, g_ref, p_ref, first_ref, second_ref,
    a_out, a_in, g_out, g_in, p_out, p_in, p_all,
    part_z, part_x,
    z_up, z_down, xa_up, xa_down, xb_up, xb_down,
    zx_up, zx_down, sa_up, sa_down, sb_up, sb_down,
    y_z, y_x, grad, grad_own, w_all, grad_all,
    proj_part, proj_x, proj_z, proj_all, stats, scale_all,
    send_sems, recv_sems, load_sems,
):
    xk, zk, yk, ck = (lax.axis_index(name) for name in FSDP)
    island = lax.axis_index(ISLAND)
    nx, nz = lax.axis_size(X), lax.axis_size(Z)
    ni = lax.axis_size(ISLAND)
    lanes = Lanes(send_sems, recv_sems)
    other_c, other_y = 1 - ck, 1 - yk
    quad = yk * 2 + ck
    half = g_ref.shape[1] // 2
    depth = first_ref.shape[0]
    rows = p_ref.shape[0]
    height = part_z.shape[2]
    mine = pl.ds(pl.multiple_of(ck * half, half), half)
    theirs = pl.ds(pl.multiple_of(other_c * half, half), half)
    here = pl.ds(pl.multiple_of((xk * 2 + yk) * depth, depth), depth)

    def near(by_x, by_y, by_c=0):
        peer = {}
        if by_x:
            peer[X] = turn(X, by_x)
        if by_y:
            peer[Y] = other_y
        if by_c:
            peer[C] = other_c
        return peer

    moves = [
        (g_hbm, g_ref), (a_hbm, a_ref), (p_hbm, p_ref),
        (w_hbm, w_all.at[island]),
        (first_hbm.at[here, mine], first_ref), (second_hbm.at[here, mine], second_ref),
    ]
    loads = [
        pltpu.make_async_copy(src, dst, load_sems.at[at])
        for at, (src, dst) in enumerate(moves)
    ]
    for load in loads:
        load.start()

    barrier = pltpu.get_barrier_semaphore()
    around = [
        near(i % nx, i // nx % 2, i // (2 * nx)) for i in range(1, 4 * nx)
    ]
    partners = around + [{Z: turn(Z, 1)}, {Z: turn(Z, -1)}]
    partners += [{ISLAND: turn(ISLAND, by)} for by in range(1, ni)]
    for partner in partners:
        pl.semaphore_signal(barrier, inc=1, device_id=partner, device_id_type=MESH_ID)
    loads[0].wait()
    g_out[...] = g_ref[:, theirs].astype(F32)
    loads[1].wait()
    a_out[...] = a_ref[...].astype(F32)
    loads[2].wait()
    p_out[...] = p_ref[...].astype(F32)
    pl.semaphore_wait(barrier, len(partners))

    wide = 11 * LANES
    spans = [slice(at, at + wide) for at in range(0, a_ref.shape[1], wide)]
    got_g = lanes.send(g_out, g_in, **{C: other_c})
    got_a = [lanes.send(a_out.at[:, at], a_in.at[:, at], **{C: other_c}) for at in spans]
    got_p = [
        lanes.send(p_out, p_in.at[quad], **near(0, y, c)) for y, c in ((0, 1), (1, 0), (1, 1))
    ]
    got_w = [
        lanes.send(w_hbm, w_all.at[island], **{ISLAND: turn(ISLAND, by)})
        for by in range(1, ni)
    ]

    def product(a, g, span, add):
        count = wide // height
        lhs = a[:, span].astype(jnp.bfloat16)
        out = lax.dot_general(lhs, g, (((0,), (0,)), ((), ())), preferred_element_type=F32)
        out = out.reshape(count, height, half)
        block = span.start // height
        done = 0
        while done < count:
            x, z = divmod(block + done, nz)
            take = min(nz - z, count - done)
            for ref, cols in ((part_z, slice(0, LANES)), (part_x, slice(LANES, half))):
                piece = out[done : done + take, :, cols]
                if add:
                    piece = ref[x, z : z + take] + piece
                ref[x, z : z + take] = piece
            done += take

    for span in spans:
        product(a_ref, g_ref[:, mine], span, False)
    p_in[quad] = p_out[...]
    got_g.wait_recv()
    for copy, span in zip(got_a, spans):
        copy.wait_recv()
        product(a_in, g_in[...].astype(jnp.bfloat16), span, True)

    up_z, up_x = nz // 2, nx // 2
    cut = xa_up.shape[3]
    both = ((1, 0), (-1, 1))
    chain_z, chain_a, chain_b = [], [], []
    for sub in range(nx):
        block = lambda d, sub=sub: part_z.at[sub, d]
        for way, slots in ((1, z_up), (-1, z_down)):
            less = int((way == 1) == (sub % 2 == 1))
            chain_z.append(chain(lanes, Z, up_z - less, way, block, slots.at[sub]))
    for chains, up, down, span in (
        (chain_a, xa_up, xa_down, slice(0, cut)),
        (chain_b, xb_up, xb_down, slice(cut, height)),
    ):
        for sub in range(2):
            lead = slice(sub * (nz // 2), (sub + 1) * (nz // 2))
            block = lambda d, lead=lead, span=span: part_x.at[d, lead, span]
            for way, slots in ((1, up), (-1, down)):
                less = int((way == 1) == (sub == 1))
                chains.append(chain(lanes, X, up_x - less, way, block, slots.at[sub]))
    block_a = lambda d: part_x.at[xk, d, slice(0, cut)]
    block_b = lambda d: part_x.at[xk, d, slice(cut, height)]
    block_z = lambda d: part_z.at[d, zk]
    last_a = [
        chain(lanes, Z, up_z - less, way, block_a, slots)
        for (way, less), slots in zip(both, (sa_up, sa_down))
    ]
    last_b = [
        chain(lanes, Z, up_z - 1 + less, way, block_b, slots)
        for (way, less), slots in zip(both, (sb_up, sb_down))
    ]
    last_z = [
        chain(lanes, X, up_x - less, way, block_z, slots)
        for (way, less), slots in zip(both, (zx_up, zx_down))
    ]
    order = [
        chain_z, chain_a, chain_z, chain_a, chain_b, chain_z,
        chain_a, last_a, chain_b, chain_z, last_a, chain_z, last_a,
        chain_b, last_b, chain_z, last_a, last_b, chain_z,
        last_z, last_a, last_b, last_z, last_a, last_b, last_z,
    ]
    for chains in order:
        advance(chains)
    got_yz = lanes.send(part_z.at[xk, zk], y_z, **{Y: other_y})
    for copy in got_p:
        copy.wait_recv()
    for j in range(4):
        p_all[j * rows : (j + 1) * rows, :] = p_in[j]
    advance(last_a)
    for _ in range(3):
        advance(last_b)

    proj_part[...] = lax.dot_general(
        p_all[...],
        jnp.concatenate([part_z[xk, zk], part_x[xk, zk]], axis=1),
        (((0,), (0,)), ((), ())),
        precision=lax.Precision.HIGHEST,
        preferred_element_type=F32,
    ).reshape(proj_part.shape)
    got_x = []
    for i in range(1, 2 * nx):
        by_x, by_y = i % nx, i // nx
        to_x = turn(X, by_x)
        to_y = other_y if by_y else yk
        got_x.append(
            lanes.send(proj_part.at[to_x, to_y], proj_x.at[i - 1], **near(by_x, by_y))
        )

    got_yx = lanes.send(part_x.at[xk, zk], y_x, **{Y: other_y})
    own = proj_part[xk, yk]
    for i, copy in enumerate(got_x):
        copy.wait_recv()
        own = own + proj_x[i]
    proj_z[zk] = own

    ups, downs = [], []
    for step in range(up_z):
        for way, held, last in ((1, ups, up_z), (-1, downs, up_z - 1)):
            if step >= last:
                continue
            if held:
                held[-1].wait_recv()
            source = proj_z.at[turn(Z, -way * step)]
            held.append(lanes.send(source, source, **{Z: turn(Z, way)}))
        if step == 0:
            got_yz.wait_recv()
            got_yx.wait_recv()
            grad[:, mine] = jnp.concatenate(
                [part_z[xk, zk] + y_z[...], part_x[xk, zk] + y_x[...]], axis=1
            )
            got_grad = lanes.send(grad.at[:, mine], grad.at[:, mine], **{C: other_c})
        if step == 1:
            got_grad.wait_recv()
            for j in range(4):
                @pl.when(quad == j)
                def _(j=j):
                    grad_own[...] = grad[j * rows : (j + 1) * rows, :]
            got_gi = [
                lanes.send(grad_own, grad_all.at[island], **{ISLAND: turn(ISLAND, by)})
                for by in range(1, ni)
            ]
    grad_all[island] = grad_own[...]
    for load in loads[3:]:
        load.wait()
    ups[-1].wait_recv()
    downs[-1].wait_recv()
    block = proj_z[0]
    for z in range(1, nz):
        block = block + proj_z[z]
    new_first = first_decay * first_ref[...] + (1.0 - first_decay) * block
    new_second = second_decay * second_ref[...] + (1.0 - second_decay) * block * block
    adapted = new_first / first_fix / (jnp.sqrt(new_second / second_fix) + epsilon)
    place = (ck * nx + xk) * 2 + yk
    stats[place, 0:1] = jnp.sum(adapted * adapted, axis=0, keepdims=True)
    stats[place, 1:2] = jnp.sum(block * block, axis=0, keepdims=True)
    got_stats = [lanes.send(stats.at[place], stats.at[place], **peer) for peer in around]
    proj_all[xk, yk, :, mine] = block
    got_proj = []
    for by in range(1, nx):
        spot = proj_all.at[xk, yk, :, mine]
        got_proj.append(lanes.send(spot, spot, **{X: turn(X, by)}))
    for copy in got_stats:
        copy.wait_recv()
    for core in range(2):
        sums = stats[2 * nx * core]
        for i in range(1, 2 * nx):
            sums = sums + stats[2 * nx * core + i]
        sums = sums / RANK
        scale_all[island, :, core * half : (core + 1) * half] = jnp.sqrt(
            sums[0:1]
        ) / jnp.sqrt(sums[1:2] + 1e-06)
    got_si = [
        lanes.send(
            scale_all.at[island], scale_all.at[island], **{ISLAND: turn(ISLAND, by)}
        )
        for by in range(1, ni)
    ]

    for copy in got_proj:
        copy.wait_recv()
    spot = proj_all.at[:, yk, :, mine]
    got_far = lanes.send(spot, spot, **{Y: other_y})
    got_close = lanes.send(spot, spot, **{C: other_c})
    for copy in got_w + got_gi:
        copy.wait_recv()
    weights = w_all[0]
    for i in range(1, ni):
        weights = weights + w_all[i]
    weights = weights.reshape(rows, grad_own.shape[1])
    got_far.wait_recv()
    spot = proj_all.at[:, other_y, :, mine]
    got_last = lanes.send(spot, spot, **{C: other_c})
    for copy in got_si:
        copy.wait_recv()
    moved = None
    for i in range(ni):
        step = inner_rate * grad_all[i] * scale_all[i]
        moved = step if moved is None else moved + step
    total_ref[...] = weights - moved
    got_close.wait_recv()
    got_last.wait_recv()
    proj_ref[...] = proj_all[...].reshape(proj_ref.shape)
    for copy in lanes.started:
        copy.wait_send()


def exchange(a, g, p, first, second, w):
    tokens, features = a.shape
    cols = g.shape[1]
    half = cols // 2
    rows = p.shape[0]
    nx, nz, ni = lax.axis_size(X), lax.axis_size(Z), lax.axis_size(ISLAND)
    quad = 4 * rows
    cut = quad // 16 * 8 + 8
    ups, upx = nz // 2, nx // 2
    vmem = lambda *shape: pltpu.VMEM(shape, F32)
    depth = RANK // nx // 2
    scratch = [
        pltpu.VMEM(a.shape, a.dtype), pltpu.VMEM(g.shape, g.dtype), pltpu.VMEM(p.shape, p.dtype),
        vmem(depth, half), vmem(depth, half),
        vmem(tokens, features), vmem(tokens, features),
        vmem(tokens, half), vmem(tokens, half),
        vmem(rows, RANK), vmem(4, rows, RANK), vmem(quad, RANK),
        vmem(nx, nz, quad, LANES), vmem(nx, nz, quad, LANES),
        vmem(nx, ups, quad, LANES), vmem(nx, ups, quad, LANES),
        vmem(2, upx, nz // 2, cut, LANES), vmem(2, upx, nz // 2, cut, LANES),
        vmem(2, upx, nz // 2, quad - cut, LANES), vmem(2, upx, nz // 2, quad - cut, LANES),
        vmem(upx, quad, LANES), vmem(upx, quad, LANES),
        vmem(ups, cut, LANES), vmem(ups, cut, LANES),
        vmem(ups, quad - cut, LANES), vmem(ups, quad - cut, LANES),
        vmem(quad, LANES), vmem(quad, LANES),
        vmem(quad, cols), vmem(rows, cols),
        vmem(ni, *w.shape), vmem(ni, rows, cols),
        vmem(nx, 2, depth, half), vmem(2 * nx - 1, depth, half), vmem(nz, depth, half),
        vmem(nx, 2, depth, cols), vmem(4 * nx, 2, half), vmem(ni, 1, cols),
        pltpu.SemaphoreType.DMA((150,)),
        pltpu.SemaphoreType.DMA((150,)),
        pltpu.SemaphoreType.DMA((6,)),
    ]
    return pl.pallas_call(
        comm_kernel,
        name="exchange",
        out_shape=(
            jax.ShapeDtypeStruct((RANK, cols), F32),
            jax.ShapeDtypeStruct((rows, cols), F32),
        ),
        in_specs=[pl.BlockSpec(memory_space=pltpu.HBM)] * 6,
        out_specs=(pl.BlockSpec(memory_space=pltpu.VMEM),) * 2,
        scratch_shapes=scratch,
        compiler_params=pltpu.CompilerParams(
            collective_id=0, has_side_effects=True, vmem_limit_bytes=67043328
        ),
    )(a, g, p, first, second, w)


def body(
    activations,
    out_grads,
    projection,
    first_moment,
    second_moment,
    inner_weights,
    global_weights,
    outer_momentum,
):
    projected, stepped_sum = exchange(
        activations[0],
        out_grads[0],
        projection,
        first_moment[0, 0],
        second_moment[0, 0],
        inner_weights.reshape(-1, 1, inner_weights.shape[2]),
    )
    new_first = first_decay * first_moment[0, 0] + (1.0 - first_decay) * projected
    new_second = (
        second_decay * second_moment[0, 0] + (1.0 - second_decay) * projected * projected
    )
    island_count = lax.axis_size(ISLAND)
    pseudo_grad = global_weights - stepped_sum / island_count
    new_momentum = outer_beta * outer_momentum + pseudo_grad
    weights_next = (
        global_weights - outer_rate * (pseudo_grad + outer_beta * new_momentum)
    ).astype(jnp.bfloat16)
    block_cols = global_weights.shape[1] // island_count
    weights_block = lax.dynamic_slice_in_dim(
        weights_next, lax.axis_index(ISLAND) * block_cols, block_cols, 1
    )
    return (weights_block, new_momentum, new_first[None, None], new_second[None, None])


def solution(mesh):
    torus = Mesh(
        mesh.devices.reshape(4, 12, 2, 2, mesh.shape["island"]),
        (*FSDP, ISLAND),
    )
    placed = (
        P(ISLAND, FSDP, None),
        P(ISLAND, FSDP, None),
        P(FSDP, None),
        P(ISLAND, None, None, None),
        P(ISLAND, None, None, None),
        P(ISLAND, FSDP, None),
        P(FSDP, None),
        P(FSDP, None),
    )
    return jax.shard_map(
        body,
        mesh=torus,
        in_specs=placed,
        out_specs=(
            P(FSDP, ISLAND),
            P(FSDP, None),
            P(ISLAND, None, None, None),
            P(ISLAND, None, None, None),
        ),
        check_vma=False,
    )
```

time: 114 us -> 116 us (1.018)
  local copies, waits for them, and re-layouts: 5.74 us -> 0.01 us
  Pallas kernels: 106 us -> 110 us
  other arithmetic: 1.79 us -> 4.71 us
    unnamed x17 -> x2, local copies, waits for them, and re-layouts: 5.74 us -> 0.01 us
    pallas_call x1, Pallas kernels: 106 us -> 110 us  [exchange(): pl.pallas_call(comm_kernel, name='exchange', out_shape=(jax.ShapeDtypeStr...]
    broadcast_in_dim x1, other arithmetic: 1.16 us -> 2.51 us  [body(): new_second[None, None]]
where the time goes in v2:
time: 116 us; the launch traced here: 115 us
  Pallas kernels  110 us (95%)
  other arithmetic  4.71 us (4%)
    pallas_call x1, Pallas kernels, exchange(): pl.pallas_call(comm_kernel, name='exchange', out_shape=(jax.ShapeDtypeStr...  110 us
    broadcast_in_dim x1, other arithmetic, body(): new_second[None, None]  2.51 us

profile of v2, /device:TPU:1, one launch (start us, length us, event | category | flops | bytes accessed | tf_op | source)
XLA Modules:
  0.0 115.5 jit_solution(5163449005918285005)
XLA Ops:
  0.6 110.1 %exchange.1 = (f32[256,512]{1,0:T(8,128)}, f32[22,512]{1,0:T(8,128)}) custom-call(bf16[128,4224]{1,0:T(8,128)(2,1)} %bitcast.13, bf16[128,512]{1,0:T(8,128)(2,1)} %bitcast.14, bf16[22,256]{1,0:T(8,128)(2,1)} %p_hbm.1, f32[256,512]{1,0:T(8,128)} %bitcast.11, f32[256,512]{1,0:T(8,128)} %bitcast.12, f32[22,1,512]{2,1,0:T(1,128)} %bitcast.15), custom_call_target="tpu_custom_call" | custom-call | tf_op jit(solution)/shard_map/exchange/pallas_call | solution.py:374
  110.8 0.9 multiply_add_fusion
  111.6 0.0 copy-start
  111.6 1.3 %fusion.2 = bf16[22,128]{1,0:T(8,128)(2,1)} fusion(f32[22,512]{1,0:T(8,128)} %param.14, s32[]{:T(128)S(6)} %select_n.3, f32[22,512]{1,0:T(8,128)S(1)} %get-tuple-element.9, f32[22,512]{1,0:T(8,128)S(1)} %get-tuple-element.8), kind=kLoop, calls=%fused_computation.7 | loop fusion | flops 14080 | bytes 39428 | tf_op jit(solution)/shard_map/convert_element_type | solution.py:417
  113.0 2.5 %fusion.1 = (f32[1,1,256,512]{3,2,1,0:T(8,128)}, f32[1,1,256,512]{3,2,1,0:T(8,128)}) fusion(f32[256,512]{1,0:T(8,128)} %get-tuple-element.7, f32[1,1,256,512]{3,2,1,0:T(8,128)} %param.12, f32[1,1,256,512]{3,2,1,0:T(8,128)} %param.11), kind=kLoop, calls=%fused_computation.2 | loop fusion | flops 917504 | bytes 2621440 | tf_op jit(solution)/shard_map/broadcast_in_dim | solution.py:422
  115.5 0.0 copy-done
Async XLA Ops:
  111.6 3.9 %copy-start = (f32[22,512]{1,0:T(8,128)}, f32[22,512]{1,0:T(8,128)S(1)}, u32[]{:S(2)}) copy-start(f32[22,512]{1,0:T(8,128)S(1)} %get-tuple-element.8) | copy-start | bytes 135172

commit v3 on v2

--- a/solution.py
+++ b/solution.py
@@ -13,6 +13,11 @@
 ISLAND = "island"
 FSDP = (X, Z, Y, C)
 LANES = 128
+RING_ORDER = (
+    "iljkmpnoadehbcfgadehilbcgfajkdehcbmpgfadonehcbgi",
+    "lqrfadehmptscbrgqfadehstcbrgqfadehuvstqrstuvqrst",
+    "qrustqt",
+)
 MESH_ID = pl.DeviceIdType.MESH
 F32 = jnp.float32
 
@@ -207,22 +212,19 @@
         chain(lanes, X, up_x - less, way, block_z, slots)
         for (way, less), slots in zip(both, (zx_up, zx_down))
     ]
-    order = [
-        chain_z, chain_a, chain_z, chain_a, chain_b, chain_z,
-        chain_a, last_a, chain_b, chain_z, last_a, chain_z, last_a,
-        chain_b, last_b, chain_z, last_a, last_b, chain_z,
-        last_z, last_a, last_b, last_z, last_a, last_b, last_z,
-    ]
-    for chains in order:
-        advance(chains)
+    every = chain_z + chain_a + chain_b + last_a + last_b + last_z
+    for letter in "".join(RING_ORDER):
+        at = ord(letter) - ord("a")
+        advance([every[at]])
+    for chains in (chain_z, chain_a, chain_b, last_a, last_b, last_z):
+        for _ in range(up_z + 1):
+            advance(chains)
     got_yz = lanes.send(part_z.at[xk, zk], y_z, **{Y: other_y})
+    got_yx = lanes.send(part_x.at[xk, zk], y_x, **{Y: other_y})
     for copy in got_p:
         copy.wait_recv()
     for j in range(4):
         p_all[j * rows : (j + 1) * rows, :] = p_in[j]
-    advance(last_a)
-    for _ in range(3):
-        advance(last_b)
 
     proj_part[...] = lax.dot_general(
         p_all[...],
@@ -240,7 +242,12 @@
             lanes.send(proj_part.at[to_x, to_y], proj_x.at[i - 1], **near(by_x, by_y))
         )
 
-    got_yx = lanes.send(part_x.at[xk, zk], y_x, **{Y: other_y})
+    got_yz.wait_recv()
+    got_yx.wait_recv()
+    grad[:, mine] = jnp.concatenate(
+        [part_z[xk, zk] + y_z[...], part_x[xk, zk] + y_x[...]], axis=1
+    )
+    got_grad = lanes.send(grad.at[:, mine], grad.at[:, mine], **{C: other_c})
     own = proj_part[xk, yk]
     for i, copy in enumerate(got_x):
         copy.wait_recv()
@@ -256,14 +263,7 @@
                 held[-1].wait_recv()
             source = proj_z.at[turn(Z, -way * step)]
             held.append(lanes.send(source, source, **{Z: turn(Z, way)}))
-        if step == 0:
-            got_yz.wait_recv()
-            got_yx.wait_recv()
-            grad[:, mine] = jnp.concatenate(
-                [part_z[xk, zk] + y_z[...], part_x[xk, zk] + y_x[...]], axis=1
-            )
-            got_grad = lanes.send(grad.at[:, mine], grad.at[:, mine], **{C: other_c})
-        if step == 1:
+        if step == 2:
             got_grad.wait_recv()
             for j in range(4):
                 @pl.when(quad == j)
@@ -290,9 +290,9 @@
     got_stats = [lanes.send(stats.at[place], stats.at[place], **peer) for peer in around]
     proj_all[xk, yk, :, mine] = block
     got_proj = []
-    for by in range(1, nx):
+    for i in range(1, 2 * nx):
         spot = proj_all.at[xk, yk, :, mine]
-        got_proj.append(lanes.send(spot, spot, **{X: turn(X, by)}))
+        got_proj.append(lanes.send(spot, spot, **near(i % nx, i // nx)))
     for copy in got_stats:
         copy.wait_recv()
     for core in range(2):
@@ -312,8 +312,7 @@
 
     for copy in got_proj:
         copy.wait_recv()
-    spot = proj_all.at[:, yk, :, mine]
-    got_far = lanes.send(spot, spot, **{Y: other_y})
+    spot = proj_all.at[:, :, :, mine]
     got_close = lanes.send(spot, spot, **{C: other_c})
     for copy in got_w + got_gi:
         copy.wait_recv()
@@ -321,9 +320,6 @@
     for i in range(1, ni):
         weights = weights + w_all[i]
     weights = weights.reshape(rows, grad_own.shape[1])
-    got_far.wait_recv()
-    spot = proj_all.at[:, other_y, :, mine]
-    got_last = lanes.send(spot, spot, **{C: other_c})
     for copy in got_si:
         copy.wait_recv()
     moved = None
@@ -332,7 +328,6 @@
         moved = step if moved is None else moved + step
     total_ref[...] = weights - moved
     got_close.wait_recv()
-    got_last.wait_recv()
     proj_ref[...] = proj_all[...].reshape(proj_ref.shape)
     for copy in lanes.started:
         copy.wait_send()
@@ -382,9 +377,9 @@
         out_specs=(pl.BlockSpec(memory_space=pltpu.VMEM),) * 2,
         scratch_shapes=scratch,
         compiler_params=pltpu.CompilerParams(
-            collective_id=0, has_side_effects=True, vmem_limit_bytes=67043328
+            collective_id=0, has_side_effects=True, vmem_limit_bytes=40 << 20
         ),
-    )(a, g, p, first, second, w)
+    )(*(pltpu.with_memory_space_constraint(v, pltpu.HBM) for v in (a, g, p, first, second, w)))
 
 
 def body(

time: 116 us -> 102 us (0.88)
  Pallas kernels: 110 us -> 99.1 us
  other arithmetic: 4.71 us -> 1.79 us
    pallas_call x1, Pallas kernels: 110 us -> 99.1 us  [exchange(): pl.pallas_call(comm_kernel, name='exchange', out_shape=(jax.ShapeDtypeStr...]
    broadcast_in_dim x1, other arithmetic: 2.51 us -> 1.16 us  [body(): new_second[None, None]]
where the time goes in v3:
time: 102 us
  Pallas kernels  99.1 us (97%)
  other arithmetic  1.79 us (2%)
    pallas_call x1, Pallas kernels, exchange(): pl.pallas_call(comm_kernel, name='exchange', out_shape=(jax.ShapeDtypeStr...  99.1 us

profile of v3, /device:TPU:1, one launch (start us, length us, event | category | flops | bytes accessed | tf_op | source)
XLA Modules:
  0.0 101.6 jit_solution(13508841168590822705)
XLA Ops:
  0.6 0.0 copy-start.2
  0.6 0.0 copy-start.4
  0.7 0.0 copy-start
  0.7 0.0 copy-start.1
  0.7 99.1 %exchange.1 = (f32[256,512]{1,0:T(8,128)S(1)}, f32[22,512]{1,0:T(8,128)S(1)}) custom-call(bf16[128,4224]{1,0:T(8,128)(2,1)} %bitcast.13, bf16[128,512]{1,0:T(8,128)(2,1)} %bitcast.14, bf16[22,256]{1,0:T(8,128)(2,1)} %p_hbm.1, f32[256,512]{1,0:T(8,128)} %bitcast.11, f32[256,512]{1,0:T(8,128)} %bitcast.12, f32[22,1,512]{2,1,0:T(1,128)} %bitcast.15), custom_call_target="tpu_custom_call" | custom-call | tf_op jit(solution)/shard_map/exchange/pallas_call | solution.py:369
  99.7 0.0 copy-done.2
  99.8 0.0 copy-done.4
  99.8 0.0 copy-start.3
  99.8 0.6 fusion.2
  100.4 0.0 copy-done
  100.4 0.0 copy-done.1
  100.4 1.2 %fusion.1 = (f32[1,1,256,512]{3,2,1,0:T(8,128)}, f32[1,1,256,512]{3,2,1,0:T(8,128)}) fusion(f32[256,512]{1,0:T(8,128)S(1)} %get-tuple-element.7, f32[1,1,256,512]{3,2,1,0:T(8,128)S(1)} %copy-done.1, f32[1,1,256,512]{3,2,1,0:T(8,128)S(1)} %copy-done), kind=kLoop, calls=%fused_computation.2 | loop fusion | flops 917504 | bytes 2621440 | tf_op jit(solution)/shard_map/broadcast_in_dim | solution.py:417
  101.6 0.0 copy-done.3
  (1 shorter events, 0.0 us)
Async XLA Ops:
  0.6 99.1 %copy-start.2 = (f32[22,512]{1,0:T(8,128)S(1)}, f32[22,512]{1,0:T(8,128)}, u32[]{:S(2)}) copy-start(f32[22,512]{1,0:T(8,128)} %param.14) | copy-start | bytes 135172
  0.6 99.1 %copy-start.4 = (f32[22,512]{1,0:T(8,128)S(1)}, f32[22,512]{1,0:T(8,128)}, u32[]{:S(2)}) copy-start(f32[22,512]{1,0:T(8,128)} %param.15) | copy-start | bytes 135172
  0.7 99.8 %copy-start = (f32[1,1,256,512]{3,2,1,0:T(8,128)S(1)}, f32[1,1,256,512]{3,2,1,0:T(8,128)}, u32[]{:S(2)}) copy-start(f32[1,1,256,512]{3,2,1,0:T(8,128)} %param.11) | copy-start | bytes 1572868
  0.7 99.8 %copy-start.1 = (f32[1,1,256,512]{3,2,1,0:T(8,128)S(1)}, f32[1,1,256,512]{3,2,1,0:T(8,128)}, u32[]{:S(2)}) copy-start(f32[1,1,256,512]{3,2,1,0:T(8,128)} %param.12) | copy-start | bytes 1572868
  99.8 1.8 %copy-start.3 = (f32[22,512]{1,0:T(8,128)}, f32[22,512]{1,0:T(8,128)S(1)}, u32[]{:S(2)}) copy-start(f32[22,512]{1,0:T(8,128)S(1)} %get-tuple-element.8) | copy-start | bytes 135172

commit v4 on v3

--- a/solution.py
+++ b/solution.py
@@ -14,9 +14,9 @@
 FSDP = (X, Z, Y, C)
 LANES = 128
 RING_ORDER = (
-    "iljkmpnoadehbcfgadehilbcgfajkdehcbmpgfadonehcbgi",
-    "lqrfadehmptscbrgqfadehstcbrgqfadehuvstqrstuvqrst",
-    "qrustqt",
+    "iljkmpnoehfgababcdabehilfgcdabkjehgfmpcdabonehgf",
+    "cdilqtrsahefmpuxvwdgtrcqshefuxwvgdqtsrehyzuxwvqt",
+    "srxuwvqytzsrxuwvqtsryxuwvqtxu",
 )
 MESH_ID = pl.DeviceIdType.MESH
 F32 = jnp.float32
@@ -173,10 +173,6 @@
     for span in spans:
         product(a_ref, g_ref[:, mine], span, False)
     p_in[quad] = p_out[...]
-    got_g.wait_recv()
-    for copy, span in zip(got_a, spans):
-        copy.wait_recv()
-        product(a_in, g_in[...].astype(jnp.bfloat16), span, True)
 
     up_z, up_x = nz // 2, nx // 2
     cut = xa_up.shape[3]
@@ -197,26 +193,33 @@
             for way, slots in ((1, up), (-1, down)):
                 less = int((way == 1) == (sub == 1))
                 chains.append(chain(lanes, X, up_x - less, way, block, slots.at[sub]))
-    block_a = lambda d: part_x.at[xk, d, slice(0, cut)]
-    block_b = lambda d: part_x.at[xk, d, slice(cut, height)]
     block_z = lambda d: part_z.at[d, zk]
-    last_a = [
-        chain(lanes, Z, up_z - less, way, block_a, slots)
-        for (way, less), slots in zip(both, (sa_up, sa_down))
-    ]
-    last_b = [
-        chain(lanes, Z, up_z - 1 + less, way, block_b, slots)
-        for (way, less), slots in zip(both, (sb_up, sb_down))
-    ]
+    last_x = []
+    for start, stop, up, down in ((0, cut, sa_up, sa_down), (cut, height, sb_up, sb_down)):
+        middle = start + -(-(stop - start) // 16) * 8
+        for span in (slice(start, middle), slice(middle, stop)):
+            less = len(last_x) // 2 % 2
+            inner = slice(span.start - start, span.stop - start)
+            block = lambda d, span=span: part_x.at[xk, d, span]
+            last_x.append(chain(lanes, Z, up_z - less, 1, block, up.at[:, inner]))
+            last_x.append(chain(lanes, Z, up_z - 1 + less, -1, block, down.at[:, inner]))
     last_z = [
         chain(lanes, X, up_x - less, way, block_z, slots)
         for (way, less), slots in zip(both, (zx_up, zx_down))
     ]
-    every = chain_z + chain_a + chain_b + last_a + last_b + last_z
+    got_g.wait_recv()
+    ready = 0
+    for copy, span in zip(got_a, spans):
+        copy.wait_recv()
+        product(a_in, g_in[...].astype(jnp.bfloat16), span, True)
+        while ready < nx // 2 and (ready + 1) * nz * height <= span.stop:
+            advance(chain_z[2 * ready : 2 * ready + 2])
+            ready += 1
+    every = chain_z + chain_a + chain_b + last_x + last_z
     for letter in "".join(RING_ORDER):
         at = ord(letter) - ord("a")
         advance([every[at]])
-    for chains in (chain_z, chain_a, chain_b, last_a, last_b, last_z):
+    for chains in (chain_z, chain_a, chain_b, last_x, last_z):
         for _ in range(up_z + 1):
             advance(chains)
     got_yz = lanes.send(part_z.at[xk, zk], y_z, **{Y: other_y})
@@ -254,16 +257,18 @@
         own = own + proj_x[i]
     proj_z[zk] = own
 
-    ups, downs = [], []
+    pieces = [slice(at, at + 8) for at in range(0, depth, 8)]
+    ups, downs = [None] * len(pieces), [None] * len(pieces)
     for step in range(up_z):
-        for way, held, last in ((1, ups, up_z), (-1, downs, up_z - 1)):
-            if step >= last:
-                continue
-            if held:
-                held[-1].wait_recv()
-            source = proj_z.at[turn(Z, -way * step)]
-            held.append(lanes.send(source, source, **{Z: turn(Z, way)}))
-        if step == 2:
+        for at, piece in enumerate(pieces):
+            for way, held, last in ((1, ups, up_z), (-1, downs, up_z - 1)):
+                if step >= last:
+                    continue
+                if step:
+                    held[at].wait_recv()
+                source = proj_z.at[turn(Z, -way * step), piece]
+                held[at] = lanes.send(source, source, **{Z: turn(Z, way)})
+        if step == min(2, up_z - 1):
             got_grad.wait_recv()
             for j in range(4):
                 @pl.when(quad == j)
@@ -276,8 +281,8 @@
     grad_all[island] = grad_own[...]
     for load in loads[3:]:
         load.wait()
-    ups[-1].wait_recv()
-    downs[-1].wait_recv()
+    for copy in ups + downs:
+        copy.wait_recv()
     block = proj_z[0]
     for z in range(1, nz):
         block = block + proj_z[z]
@@ -362,8 +367,8 @@
         vmem(ni, *w.shape), vmem(ni, rows, cols),
         vmem(nx, 2, depth, half), vmem(2 * nx - 1, depth, half), vmem(nz, depth, half),
         vmem(nx, 2, depth, cols), vmem(4 * nx, 2, half), vmem(ni, 1, cols),
-        pltpu.SemaphoreType.DMA((150,)),
-        pltpu.SemaphoreType.DMA((150,)),
+        pltpu.SemaphoreType.DMA((200,)),
+        pltpu.SemaphoreType.DMA((200,)),
         pltpu.SemaphoreType.DMA((6,)),
     ]
     return pl.pallas_call(

time: 102 us -> 103 us (level)
    pallas_call x1, Pallas kernels: 99.1 us -> 100 us  [exchange(): pl.pallas_call(comm_kernel, name='exchange', out_shape=(jax.ShapeDtypeStr...]
where the time goes in v4:
time: 103 us
  Pallas kernels  100 us (97%)
  other arithmetic  1.79 us (2%)
    pallas_call x1, Pallas kernels, exchange(): pl.pallas_call(comm_kernel, name='exchange', out_shape=(jax.ShapeDtypeStr...  100 us

profile of v4, /device:TPU:1, one launch (start us, length us, event | category | flops | bytes accessed | tf_op | source)
XLA Modules:
  0.0 103.0 jit_solution(4814969061048525228)
XLA Ops:
  0.6 0.0 copy-start.2
  0.6 0.0 copy-start.4
  0.7 0.0 copy-start
  0.7 0.0 copy-start.1
  0.7 100.5 %exchange.1 = (f32[256,512]{1,0:T(8,128)S(1)}, f32[22,512]{1,0:T(8,128)S(1)}) custom-call(bf16[128,4224]{1,0:T(8,128)(2,1)} %bitcast.13, bf16[128,512]{1,0:T(8,128)(2,1)} %bitcast.14, bf16[22,256]{1,0:T(8,128)(2,1)} %p_hbm.1, f32[256,512]{1,0:T(8,128)} %bitcast.11, f32[256,512]{1,0:T(8,128)} %bitcast.12, f32[22,1,512]{2,1,0:T(1,128)} %bitcast.15), custom_call_target="tpu_custom_call" | custom-call | tf_op jit(solution)/shard_map/exchange/pallas_call | solution.py:374
  101.2 0.0 copy-done.2
  101.2 0.0 copy-done.4
  101.2 0.0 copy-start.3
  101.2 0.6 fusion.2
  101.8 0.0 copy-done
  101.9 0.0 copy-done.1
  101.9 1.2 %fusion.1 = (f32[1,1,256,512]{3,2,1,0:T(8,128)}, f32[1,1,256,512]{3,2,1,0:T(8,128)}) fusion(f32[256,512]{1,0:T(8,128)S(1)} %get-tuple-element.7, f32[1,1,256,512]{3,2,1,0:T(8,128)S(1)} %copy-done.1, f32[1,1,256,512]{3,2,1,0:T(8,128)S(1)} %copy-done), kind=kLoop, calls=%fused_computation.2 | loop fusion | flops 917504 | bytes 2621440 | tf_op jit(solution)/shard_map/broadcast_in_dim | solution.py:422
  103.0 0.0 copy-done.3
  (1 shorter events, 0.0 us)
Async XLA Ops:
  0.6 100.5 %copy-start.2 = (f32[22,512]{1,0:T(8,128)S(1)}, f32[22,512]{1,0:T(8,128)}, u32[]{:S(2)}) copy-start(f32[22,512]{1,0:T(8,128)} %param.14) | copy-start | bytes 135172
  0.6 100.5 %copy-start.4 = (f32[22,512]{1,0:T(8,128)S(1)}, f32[22,512]{1,0:T(8,128)}, u32[]{:S(2)}) copy-start(f32[22,512]{1,0:T(8,128)} %param.15) | copy-start | bytes 135172
  0.7 101.2 %copy-start = (f32[1,1,256,512]{3,2,1,0:T(8,128)S(1)}, f32[1,1,256,512]{3,2,1,0:T(8,128)}, u32[]{:S(2)}) copy-start(f32[1,1,256,512]{3,2,1,0:T(8,128)} %param.11) | copy-start | bytes 1572868
  0.7 101.2 %copy-start.1 = (f32[1,1,256,512]{3,2,1,0:T(8,128)S(1)}, f32[1,1,256,512]{3,2,1,0:T(8,128)}, u32[]{:S(2)}) copy-start(f32[1,1,256,512]{3,2,1,0:T(8,128)} %param.12) | copy-start | bytes 1572868
  101.2 1.8 %copy-start.3 = (f32[22,512]{1,0:T(8,128)}, f32[22,512]{1,0:T(8,128)S(1)}, u32[]{:S(2)}) copy-start(f32[22,512]{1,0:T(8,128)S(1)} %get-tuple-element.8) | copy-start | bytes 135172

commit v5 on v3

--- a/solution.py
+++ b/solution.py
@@ -14,9 +14,9 @@
 FSDP = (X, Z, Y, C)
 LANES = 128
 RING_ORDER = (
-    "iljkmpnoadehbcfgadehilbcgfajkdehcbmpgfadonehcbgi",
-    "lqrfadehmptscbrgqfadehstcbrgqfadehuvstqrstuvqrst",
-    "qrustqt",
+    "iljkmpnoehfgababcdabehilfgcdabkjehgfmpcdabonehgf",
+    "cdilqrahefmptsgdrcqhefstgdqrehuvstqrsutvqrstuqrs",
+    "tqt",
 )
 MESH_ID = pl.DeviceIdType.MESH
 F32 = jnp.float32
@@ -173,10 +173,6 @@
     for span in spans:
         product(a_ref, g_ref[:, mine], span, False)
     p_in[quad] = p_out[...]
-    got_g.wait_recv()
-    for copy, span in zip(got_a, spans):
-        copy.wait_recv()
-        product(a_in, g_in[...].astype(jnp.bfloat16), span, True)
 
     up_z, up_x = nz // 2, nx // 2
     cut = xa_up.shape[3]
@@ -212,6 +208,14 @@
         chain(lanes, X, up_x - less, way, block_z, slots)
         for (way, less), slots in zip(both, (zx_up, zx_down))
     ]
+    got_g.wait_recv()
+    ready = 0
+    for copy, span in zip(got_a, spans):
+        copy.wait_recv()
+        product(a_in, g_in[...].astype(jnp.bfloat16), span, True)
+        while ready < nx // 2 and (ready + 1) * nz * height <= span.stop:
+            advance(chain_z[2 * ready : 2 * ready + 2])
+            ready += 1
     every = chain_z + chain_a + chain_b + last_a + last_b + last_z
     for letter in "".join(RING_ORDER):
         at = ord(letter) - ord("a")
@@ -226,13 +230,17 @@
     for j in range(4):
         p_all[j * rows : (j + 1) * rows, :] = p_in[j]
 
-    proj_part[...] = lax.dot_general(
-        p_all[...],
-        jnp.concatenate([part_z[xk, zk], part_x[xk, zk]], axis=1),
-        (((0,), (0,)), ((), ())),
-        precision=lax.Precision.HIGHEST,
-        preferred_element_type=F32,
-    ).reshape(proj_part.shape)
+    rest = jnp.concatenate([part_z[xk, zk], part_x[xk, zk]], axis=1)
+    sides = p_all[...].astype(jnp.bfloat16)
+    terms = None
+    for _ in range(3):
+        term = rest.astype(jnp.bfloat16)
+        rest = rest - term.astype(F32)
+        term = lax.dot_general(
+            sides, term, (((0,), (0,)), ((), ())), preferred_element_type=F32
+        )
+        terms = term if terms is None else terms + term
+    proj_part[...] = terms.reshape(proj_part.shape)
     got_x = []
     for i in range(1, 2 * nx):
         by_x, by_y = i % nx, i // nx
@@ -263,7 +271,7 @@
                 held[-1].wait_recv()
             source = proj_z.at[turn(Z, -way * step)]
             held.append(lanes.send(source, source, **{Z: turn(Z, way)}))
-        if step == 2:
+        if step == min(2, up_z - 1):
             got_grad.wait_recv()
             for j in range(4):
                 @pl.when(quad == j)

time: 102 us -> 102 us (level)
  no operation moved by 1% of the time
where the time goes in v5:
time: 102 us
  Pallas kernels  99.5 us (98%)
  other arithmetic  1.79 us (2%)
    pallas_call x1, Pallas kernels, exchange(): pl.pallas_call(comm_kernel, name='exchange', out_shape=(jax.ShapeDtypeStr...  99.5 us

profile of v5, /device:TPU:1, one launch (start us, length us, event | category | flops | bytes accessed | tf_op | source)
XLA Modules:
  0.0 102.0 jit_solution(2925528436817337688)
XLA Ops:
  0.6 0.0 copy-start.2
  0.6 0.0 copy-start.4
  0.7 0.0 copy-start
  0.7 0.0 copy-start.1
  0.7 99.5 %exchange.1 = (f32[256,512]{1,0:T(8,128)S(1)}, f32[22,512]{1,0:T(8,128)S(1)}) custom-call(bf16[128,4224]{1,0:T(8,128)(2,1)} %bitcast.13, bf16[128,512]{1,0:T(8,128)(2,1)} %bitcast.14, bf16[22,256]{1,0:T(8,128)(2,1)} %p_hbm.1, f32[256,512]{1,0:T(8,128)} %bitcast.11, f32[256,512]{1,0:T(8,128)} %bitcast.12, f32[22,1,512]{2,1,0:T(1,128)} %bitcast.15), custom_call_target="tpu_custom_call" | custom-call | tf_op jit(solution)/shard_map/exchange/pallas_call | solution.py:377
  100.2 0.0 copy-done.2
  100.2 0.0 copy-done.4
  100.2 0.0 copy-start.3
  100.2 0.6 fusion.2
  100.8 0.0 copy-done
  100.8 0.0 copy-done.1
  100.9 1.2 %fusion.1 = (f32[1,1,256,512]{3,2,1,0:T(8,128)}, f32[1,1,256,512]{3,2,1,0:T(8,128)}) fusion(f32[256,512]{1,0:T(8,128)S(1)} %get-tuple-element.7, f32[1,1,256,512]{3,2,1,0:T(8,128)S(1)} %copy-done.1, f32[1,1,256,512]{3,2,1,0:T(8,128)S(1)} %copy-done), kind=kLoop, calls=%fused_computation.2 | loop fusion | flops 917504 | bytes 2621440 | tf_op jit(solution)/shard_map/broadcast_in_dim | solution.py:425
  102.0 0.0 copy-done.3
  (1 shorter events, 0.0 us)
Async XLA Ops:
  0.6 99.5 %copy-start.2 = (f32[22,512]{1,0:T(8,128)S(1)}, f32[22,512]{1,0:T(8,128)}, u32[]{:S(2)}) copy-start(f32[22,512]{1,0:T(8,128)} %param.14) | copy-start | bytes 135172
  0.6 99.5 %copy-start.4 = (f32[22,512]{1,0:T(8,128)S(1)}, f32[22,512]{1,0:T(8,128)}, u32[]{:S(2)}) copy-start(f32[22,512]{1,0:T(8,128)} %param.15) | copy-start | bytes 135172
  0.7 100.2 %copy-start = (f32[1,1,256,512]{3,2,1,0:T(8,128)S(1)}, f32[1,1,256,512]{3,2,1,0:T(8,128)}, u32[]{:S(2)}) copy-start(f32[1,1,256,512]{3,2,1,0:T(8,128)} %param.11) | copy-start | bytes 1572868
  0.7 100.2 %copy-start.1 = (f32[1,1,256,512]{3,2,1,0:T(8,128)S(1)}, f32[1,1,256,512]{3,2,1,0:T(8,128)}, u32[]{:S(2)}) copy-start(f32[1,1,256,512]{3,2,1,0:T(8,128)} %param.12) | copy-start | bytes 1572868
  100.2 1.8 %copy-start.3 = (f32[22,512]{1,0:T(8,128)}, f32[22,512]{1,0:T(8,128)S(1)}, u32[]{:S(2)}) copy-start(f32[22,512]{1,0:T(8,128)S(1)} %get-tuple-element.8) | copy-start | bytes 135172

commit v6 on v5

--- a/solution.py
+++ b/solution.py
@@ -14,8 +14,8 @@
 FSDP = (X, Z, Y, C)
 LANES = 128
 RING_ORDER = (
-    "iljkmpnoehfgababcdabehilfgcdabkjehgfmpcdabonehgf",
-    "cdilqrahefmptsgdrcqhefstgdqrehuvstqrsutvqrstuqrs",
+    "iljkmpnoehfgadehilbcgfajkdehcbmpgfadonehcbgilqrf",
+    "adehmptscbrgqfadehstcbrgqfadehuvstqrstuvqrstqrus",
     "tqt",
 )
 MESH_ID = pl.DeviceIdType.MESH

time: 102 us -> 102 us (level)
  no operation moved by 1% of the time
where the time goes in v6:
time: 102 us
  Pallas kernels  99.1 us (97%)
  other arithmetic  1.79 us (2%)
    pallas_call x1, Pallas kernels, exchange(): pl.pallas_call(comm_kernel, name='exchange', out_shape=(jax.ShapeDtypeStr...  99.1 us

profile of v6, /device:TPU:1, one launch (start us, length us, event | category | flops | bytes accessed | tf_op | source)
XLA Modules:
  0.0 101.6 jit_solution(8374399933724307401)
XLA Ops:
  0.6 0.0 copy-start.2
  0.6 0.0 copy-start.4
  0.7 0.0 copy-start
  0.7 0.0 copy-start.1
  0.7 99.1 %exchange.1 = (f32[256,512]{1,0:T(8,128)S(1)}, f32[22,512]{1,0:T(8,128)S(1)}) custom-call(bf16[128,4224]{1,0:T(8,128)(2,1)} %bitcast.13, bf16[128,512]{1,0:T(8,128)(2,1)} %bitcast.14, bf16[22,256]{1,0:T(8,128)(2,1)} %p_hbm.1, f32[256,512]{1,0:T(8,128)} %bitcast.11, f32[256,512]{1,0:T(8,128)} %bitcast.12, f32[22,1,512]{2,1,0:T(1,128)} %bitcast.15), custom_call_target="tpu_custom_call" | custom-call | tf_op jit(solution)/shard_map/exchange/pallas_call | solution.py:377
  99.7 0.0 copy-done.2
  99.8 0.0 copy-done.4
  99.8 0.0 copy-start.3
  99.8 0.6 fusion.2
  100.4 0.0 copy-done
  100.4 0.0 copy-done.1
  100.4 1.2 %fusion.1 = (f32[1,1,256,512]{3,2,1,0:T(8,128)}, f32[1,1,256,512]{3,2,1,0:T(8,128)}) fusion(f32[256,512]{1,0:T(8,128)S(1)} %get-tuple-element.7, f32[1,1,256,512]{3,2,1,0:T(8,128)S(1)} %copy-done.1, f32[1,1,256,512]{3,2,1,0:T(8,128)S(1)} %copy-done), kind=kLoop, calls=%fused_computation.2 | loop fusion | flops 917504 | bytes 2621440 | tf_op jit(solution)/shard_map/broadcast_in_dim | solution.py:425
  101.6 0.0 copy-done.3
  (1 shorter events, 0.0 us)
Async XLA Ops:
  0.6 99.1 %copy-start.2 = (f32[22,512]{1,0:T(8,128)S(1)}, f32[22,512]{1,0:T(8,128)}, u32[]{:S(2)}) copy-start(f32[22,512]{1,0:T(8,128)} %param.14) | copy-start | bytes 135172
  0.6 99.1 %copy-start.4 = (f32[22,512]{1,0:T(8,128)S(1)}, f32[22,512]{1,0:T(8,128)}, u32[]{:S(2)}) copy-start(f32[22,512]{1,0:T(8,128)} %param.15) | copy-start | bytes 135172
  0.7 99.8 %copy-start = (f32[1,1,256,512]{3,2,1,0:T(8,128)S(1)}, f32[1,1,256,512]{3,2,1,0:T(8,128)}, u32[]{:S(2)}) copy-start(f32[1,1,256,512]{3,2,1,0:T(8,128)} %param.11) | copy-start | bytes 1572868
  0.7 99.8 %copy-start.1 = (f32[1,1,256,512]{3,2,1,0:T(8,128)S(1)}, f32[1,1,256,512]{3,2,1,0:T(8,128)}, u32[]{:S(2)}) copy-start(f32[1,1,256,512]{3,2,1,0:T(8,128)} %param.12) | copy-start | bytes 1572868
  99.8 1.8 %copy-start.3 = (f32[22,512]{1,0:T(8,128)}, f32[22,512]{1,0:T(8,128)S(1)}, u32[]{:S(2)}) copy-start(f32[22,512]{1,0:T(8,128)S(1)} %get-tuple-element.8) | copy-start | bytes 135172
